TPU v7x, 256 devices: a whole 4x4x8 slice. The times are simulated.
256 devices in a mesh: row: 64 (over z, y, core), col: 4 (over x).
Axes of the slice: x: 4, y: 4, z: 8, core: 2. Of those that a mesh axis runs over, the one named last changes fastest.
Arguments:
- rhs: float32 [7, 128, 64, 128], P(None, 'row'), may hold values from -6 to 6
- inv_diag: float32 [7, 128, 128, 128], P(None, 'row'), as said below
- lower_blocks: bfloat16 [6, 128, 16, 128, 128], P(None, 'row', 'col'), may hold values from -0.09375 to 0.09375
- col_index: int32 [6, 128, 16], P(None, 'row', 'col'), may hold values from 0 to 127, as said below
Outputs:
- solution: float32 [7, 128, 64, 128], P(None, 'row', 'col')
Inputs may be any that keep to these rules, and one draw needn't show every extreme that they name: `col_index`: at level l (1 to 6) every entry lies below 2 ** l * 2. `inv_diag`: each block is lower triangular with a positive diagonal.
All inputs are finite; a program needn't handle non-finite values.
Results may differ from a plain program's by a relative error of at most 0.003.
Values may be sent and summed in bfloat16 or wider, within the bound.
A program may use at most 64 MiB of HBM per device.

v0:
```python
import jax
import jax.numpy as jnp
from jax import lax
from jax.sharding import PartitionSpec as P


def partner(x, axis, stride):
    return lax.ppermute(x, axis, [(i, i ^ 1 << stride) for i in range(lax.axis_size(axis))])


def apply_inverse(resid, inverse):
    return jnp.einsum("nsq,nrq->nsr", resid, inverse, precision=lax.Precision.HIGHEST)


def on_device(rhs, inv_diag, lower_blocks, col_index):
    col_count = lax.axis_size("col")
    col_here = lax.axis_index("col")
    row_here = lax.axis_index("row")
    depth = lax.axis_size("row").bit_length() - 1
    share = rhs.shape[2] // col_count
    offset = col_here * share
    current = apply_inverse(rhs[0], inv_diag[0])
    results = [lax.dynamic_slice_in_dim(current, offset, share, 1)]
    for level in range(1, depth + 1):
        sendable = current.astype(jnp.bfloat16)
        subtree = sendable
        for bit in range(level):
            other = partner(subtree, "row", bit)
            upper = row_here >> bit & 1 == 1
            subtree = jnp.where(
                upper, jnp.concatenate([other, subtree], 0), jnp.concatenate([subtree, other], 0)
            )
        picked = subtree[col_index[level - 1]]
        partial_value = jnp.einsum(
            "nksq,nkrq->nsr", picked, lower_blocks[level - 1], preferred_element_type=jnp.float32
        )
        total = lax.psum(partial_value, "col")
        current = apply_inverse(rhs[level] - total, inv_diag[level])
        results.append(lax.dynamic_slice_in_dim(current, offset, share, 1))
    return jnp.stack(results, 0)


def solution(mesh):
    placed = (
        P(None, "row", None, None),
        P(None, "row", None, None),
        P(None, "row", "col", None, None),
        P(None, "row", "col"),
    )
    return jax.shard_map(
        on_device,
        mesh=mesh,
        in_specs=placed,
        out_specs=P(None, "row", "col", None),
        check_vma=False,
    )
```

profile of v0, /device:TPU:1, one launch (start us, length us, event | category | flops | bytes accessed | tf_op | source)
XLA Modules:
  0.0 488.7 jit_solution(15900296774928938731)
XLA Ops:
  6.5 1.4 fusion.41
  8.0 3.3 collective-permute-start
  11.3 1.3 slice_reduce_fusion
  13.3 1.8 convolution_bitcast_fusion.5
  15.1 44.7 %all-reduce.7.cloned.1.call-done = f32[2,64,128]{2,1,0:T(8,128)} async-done(((f32[2,64,128]{2,1,0:T(8,128)}), f32[2,64,128]{2,1,0:T(8,128)}) %all-reduce.7.cloned.1.call-update) | async-done | bytes 65552 | tf_op jit(solution)/shard_map/psum | solution.py:37
  59.8 1.3 fusion.42
  61.2 2.8 collective-permute-start.1
  64.0 0.8 collective-permute-done.1
  64.8 1.3 collective-permute-start.2
  66.1 1.9 collective-permute-done.2
  68.6 0.8 convolution_bitcast_fusion.4
  69.5 45.3 %all-reduce.9.cloned.1.call-done = f32[2,64,128]{2,1,0:T(8,128)} async-done(((f32[2,64,128]{2,1,0:T(8,128)}), f32[2,64,128]{2,1,0:T(8,128)}) %all-reduce.9.cloned.1.call-update) | async-done | bytes 65552 | tf_op jit(solution)/shard_map/psum | solution.py:37
  114.8 1.3 fusion.43
  116.1 2.8 collective-permute-start.3
  118.9 0.9 collective-permute-done.3
  119.8 1.3 collective-permute-start.4
  121.1 1.9 collective-permute-done.4
  123.0 2.8 collective-permute-start.5
  125.9 2.5 collective-permute-done.5
  129.0 0.8 convolution_bitcast_fusion.3
  129.9 46.4 %all-reduce.11.cloned.1.call-done = f32[2,64,128]{2,1,0:T(8,128)} async-done(((f32[2,64,128]{2,1,0:T(8,128)}), f32[2,64,128]{2,1,0:T(8,128)}) %all-reduce.11.cloned.1.call-update) | async-done | bytes 65552 | tf_op jit(solution)/shard_map/psum | solution.py:37
  176.4 1.3 fusion.44
  177.7 2.8 collective-permute-start.6
  180.5 0.9 collective-permute-done.6
  181.3 1.3 collective-permute-start.7
  182.6 1.9 collective-permute-done.7
  184.6 2.8 collective-permute-start.8
  187.4 2.6 collective-permute-done.8
  190.0 1.4 collective-permute-start.9
  191.5 3.9 collective-permute-done.9
  196.0 0.8 convolution_bitcast_fusion.2
  196.9 47.6 %all-reduce.13.cloned.1.call-done = f32[2,64,128]{2,1,0:T(8,128)} async-done(((f32[2,64,128]{2,1,0:T(8,128)}), f32[2,64,128]{2,1,0:T(8,128)}) %all-reduce.13.cloned.1.call-update) | async-done | bytes 65552 | tf_op jit(solution)/shard_map/psum | solution.py:37
  244.5 1.3 fusion.45
  245.8 2.8 collective-permute-start.10
  248.6 0.9 collective-permute-done.10
  249.4 1.3 collective-permute-start.11
  250.7 1.9 collective-permute-done.11
  252.7 2.8 collective-permute-start.12
  255.5 2.6 collective-permute-done.12
  258.1 1.4 collective-permute-start.13
  259.5 3.9 collective-permute-done.13
  263.5 2.3 collective-permute-start.14
  265.9 22.1 %collective-permute-done.14 = bf16[32,64,128]{2,1,0:T(8,128)(2,1)} collective-permute-done((bf16[32,64,128]{2,1,0:T(8,128)(2,1)S(1)}, bf16[32,64,128]{2,1,0:T(8,128)(2,1)}, u32[]{:S(2)}, u32[]{:S(2)}) %collective-permute-start.14) | collective-permute-done | bytes 524320 | tf_op jit(solution)/shard_map/ppermute | solution.py:8
  288.0 1.4 maximum_select_fusion.1
  289.9 0.8 convolution_bitcast_fusion.1
  290.9 45.9 %all-reduce.15.cloned.1.call-done = f32[2,64,128]{2,1,0:T(8,128)} async-done(((f32[2,64,128]{2,1,0:T(8,128)}), f32[2,64,128]{2,1,0:T(8,128)}) %all-reduce.15.cloned.1.call-update) | async-done | bytes 65552 | tf_op jit(solution)/shard_map/psum | solution.py:37
  336.8 1.3 fusion.46
  338.1 2.8 collective-permute-start.15
  340.9 0.9 collective-permute-done.15
  341.8 1.5 collective-permute-start.16
  343.2 1.9 collective-permute-done.16
  345.2 2.8 collective-permute-start.17
  348.0 2.6 collective-permute-done.17
  350.6 1.4 collective-permute-start.18
  352.0 3.9 collective-permute-done.18
  356.0 2.3 collective-permute-start.19
  358.3 22.0 %collective-permute-done.19 = bf16[32,64,128]{2,1,0:T(8,128)(2,1)S(1)} collective-permute-done((bf16[32,64,128]{2,1,0:T(8,128)(2,1)S(1)}, bf16[32,64,128]{2,1,0:T(8,128)(2,1)S(1)}, u32[]{:S(2)}, u32[]{:S(2)}) %collective-permute-start.19) | collective-permute-done | bytes 524320 | tf_op jit(solution)/shard_map/ppermute | solution.py:8
  380.6 7.1 %collective-permute-start.20 = (bf16[64,64,128]{2,1,0:T(8,128)(2,1)S(1)}, bf16[64,64,128]{2,1,0:T(8,128)(2,1)}, u32[]{:S(2)}, u32[]{:S(2)}) collective-permute-start(bf16[64,64,128]{2,1,0:T(8,128)(2,1)S(1)} %maximum_select_fusion.2), channel_id=1, source_target_pairs={{0,128},{4,132},{8,136},{12,140},{16,144},{20,148},{24,152},{28,15... | collective-permute-start | bytes 3145736 | tf_op jit(solution)/shard_map/ppermute | solution.py:8
  387.9 0.6 copy-done.1
  388.5 45.0 %collective-permute-done.20 = bf16[64,64,128]{2,1,0:T(8,128)(2,1)} collective-permute-done((bf16[64,64,128]{2,1,0:T(8,128)(2,1)S(1)}, bf16[64,64,128]{2,1,0:T(8,128)(2,1)}, u32[]{:S(2)}, u32[]{:S(2)}) %collective-permute-start.20) | collective-permute-done | bytes 1048608 | tf_op jit(solution)/shard_map/ppermute | solution.py:8
  433.5 1.9 maximum_select_fusion
  435.9 1.8 convolution_bitcast_fusion
  438.3 41.6 %all-reduce.17.cloned.1.call-done = f32[2,64,128]{2,1,0:T(8,128)} async-done(((f32[2,64,128]{2,1,0:T(8,128)}), f32[2,64,128]{2,1,0:T(8,128)}) %all-reduce.17.cloned.1.call-update) | async-done | bytes 65552 | tf_op jit(solution)/shard_map/psum | solution.py:37
  479.9 1.3 fusion.12
  (63 shorter events, 6.2 us)
Async XLA Ops:
  6.5 62.1 %copy-start = (bf16[6,2,4,128,128]{4,3,2,1,0:T(8,128)(2,1)S(1)}, bf16[6,2,4,128,128]{4,3,2,1,0:T(8,128)(2,1)}, u32[]{:S(2)}) copy-start(bf16[6,2,4,128,128]{4,3,2,1,0:T(8,128)(2,1)} %param.6) | copy-start | bytes 4718596
  6.5 53.3 %all-reduce.7.cloned.1.call-start = ((), (), s32[]{:S(2)}) async-start(), calls=%async_computation | async-start | bytes 131072 | tf_op jit(solution)/shard_map/psum | solution.py:37
  8.0 4.7 collective-permute-start
  15.1 99.7 %all-reduce.9.cloned.1.call-start = ((), (), s32[]{:S(2)}) async-start(), calls=%async_computation.1 | async-start | bytes 131072 | tf_op jit(solution)/shard_map/psum | solution.py:37
  61.2 3.6 collective-permute-start.1
  64.8 3.2 collective-permute-start.2
  69.5 106.9 %all-reduce.11.cloned.1.call-start = ((), (), s32[]{:S(2)}) async-start(), calls=%async_computation.2 | async-start | bytes 131072 | tf_op jit(solution)/shard_map/psum | solution.py:37
  116.1 3.6 collective-permute-start.3
  119.8 3.2 collective-permute-start.4
  123.0 5.4 %collective-permute-start.5 = (bf16[8,64,128]{2,1,0:T(8,128)(2,1)S(1)}, bf16[8,64,128]{2,1,0:T(8,128)(2,1)S(1)}, u32[]{:S(2)}, u32[]{:S(2)}) collective-permute-start(bf16[8,64,128]{2,1,0:T(8,128)(2,1)S(1)} %maximum_select_fusion.11), channel_id=1, source_target_pairs={{0,16},{4,20},{8,24},{12,28},{16,0},{20,4},{24,8},{28,12},{32,48},... | collective-permute-start | bytes 393224 | tf_op jit(solution)/shard_map/ppermute | solution.py:8
  129.9 114.6 %all-reduce.13.cloned.1.call-start = ((), (), s32[]{:S(2)}) async-start(), calls=%async_computation.3 | async-start | bytes 131072 | tf_op jit(solution)/shard_map/psum | solution.py:37
  177.7 3.6 collective-permute-start.6
  181.3 3.2 collective-permute-start.7
  184.6 5.4 %collective-permute-start.8 = (bf16[8,64,128]{2,1,0:T(8,128)(2,1)S(1)}, bf16[8,64,128]{2,1,0:T(8,128)(2,1)S(1)}, u32[]{:S(2)}, u32[]{:S(2)}) collective-permute-start(bf16[8,64,128]{2,1,0:T(8,128)(2,1)S(1)} %maximum_select_fusion.12), channel_id=1, source_target_pairs={{0,16},{4,20},{8,24},{12,28},{16,0},{20,4},{24,8},{28,12},{32,48},... | collective-permute-start | bytes 393224 | tf_op jit(solution)/shard_map/ppermute | solution.py:8
  190.0 5.3 %collective-permute-start.9 = (bf16[16,64,128]{2,1,0:T(8,128)(2,1)S(1)}, bf16[16,64,128]{2,1,0:T(8,128)(2,1)S(1)}, u32[]{:S(2)}, u32[]{:S(2)}) collective-permute-start(bf16[16,64,128]{2,1,0:T(8,128)(2,1)S(1)} %maximum_select_fusion.7), channel_id=1, source_target_pairs={{0,32},{4,36},{8,40},{12,44},{16,48},{20,52},{24,56},{28,60},{32,0... | collective-permute-start | bytes 786440 | tf_op jit(solution)/shard_map/ppermute | solution.py:8
  196.8 139.9 %all-reduce.15.cloned.1.call-start = ((), (), s32[]{:S(2)}) async-start(), calls=%async_computation.4 | async-start | bytes 131072 | tf_op jit(solution)/shard_map/psum | solution.py:37
  245.8 3.6 collective-permute-start.10
  249.4 3.2 collective-permute-start.11
  252.7 5.4 %collective-permute-start.12 = (bf16[8,64,128]{2,1,0:T(8,128)(2,1)S(1)}, bf16[8,64,128]{2,1,0:T(8,128)(2,1)S(1)}, u32[]{:S(2)}, u32[]{:S(2)}) collective-permute-start(bf16[8,64,128]{2,1,0:T(8,128)(2,1)S(1)} %maximum_select_fusion.13), channel_id=1, source_target_pairs={{0,16},{4,20},{8,24},{12,28},{16,0},{20,4},{24,8},{28,12},{32,48},... | collective-permute-start | bytes 393224 | tf_op jit(solution)/shard_map/ppermute | solution.py:8
  258.1 5.3 %collective-permute-start.13 = (bf16[16,64,128]{2,1,0:T(8,128)(2,1)S(1)}, bf16[16,64,128]{2,1,0:T(8,128)(2,1)S(1)}, u32[]{:S(2)}, u32[]{:S(2)}) collective-permute-start(bf16[16,64,128]{2,1,0:T(8,128)(2,1)S(1)} %maximum_select_fusion.8), channel_id=1, source_target_pairs={{0,32},{4,36},{8,40},{12,44},{16,48},{20,52},{24,56},{28,60},{32,0... | collective-permute-start | bytes 786440 | tf_op jit(solution)/shard_map/ppermute | solution.py:8
  263.5 24.5 %collective-permute-start.14 = (bf16[32,64,128]{2,1,0:T(8,128)(2,1)S(1)}, bf16[32,64,128]{2,1,0:T(8,128)(2,1)}, u32[]{:S(2)}, u32[]{:S(2)}) collective-permute-start(bf16[32,64,128]{2,1,0:T(8,128)(2,1)S(1)} %maximum_select_fusion.4), channel_id=1, source_target_pairs={{0,64},{4,68},{8,72},{12,76},{16,80},{20,84},{24,88},{28,92},{32,9... | collective-permute-start | bytes 1572872 | tf_op jit(solution)/shard_map/ppermute | solution.py:8
  290.8 189.1 %all-reduce.17.cloned.1.call-start = ((), (), s32[]{:S(2)}) async-start(), calls=%async_computation.5 | async-start | bytes 131072 | tf_op jit(solution)/shard_map/psum | solution.py:37
  338.1 3.6 collective-permute-start.15
  341.8 3.4 collective-permute-start.16
  345.2 5.4 %collective-permute-start.17 = (bf16[8,64,128]{2,1,0:T(8,128)(2,1)S(1)}, bf16[8,64,128]{2,1,0:T(8,128)(2,1)S(1)}, u32[]{:S(2)}, u32[]{:S(2)}) collective-permute-start(bf16[8,64,128]{2,1,0:T(8,128)(2,1)S(1)} %maximum_select_fusion.14), channel_id=1, source_target_pairs={{0,16},{4,20},{8,24},{12,28},{16,0},{20,4},{24,8},{28,12},{32,48},... | collective-permute-start | bytes 393224 | tf_op jit(solution)/shard_map/ppermute | solution.py:8
  350.6 5.3 %collective-permute-start.18 = (bf16[16,64,128]{2,1,0:T(8,128)(2,1)S(1)}, bf16[16,64,128]{2,1,0:T(8,128)(2,1)S(1)}, u32[]{:S(2)}, u32[]{:S(2)}) collective-permute-start(bf16[16,64,128]{2,1,0:T(8,128)(2,1)S(1)} %maximum_select_fusion.9), channel_id=1, source_target_pairs={{0,32},{4,36},{8,40},{12,44},{16,48},{20,52},{24,56},{28,60},{32,0... | collective-permute-start | bytes 786440 | tf_op jit(solution)/shard_map/ppermute | solution.py:8
  356.0 24.4 %collective-permute-start.19 = (bf16[32,64,128]{2,1,0:T(8,128)(2,1)S(1)}, bf16[32,64,128]{2,1,0:T(8,128)(2,1)S(1)}, u32[]{:S(2)}, u32[]{:S(2)}) collective-permute-start(bf16[32,64,128]{2,1,0:T(8,128)(2,1)S(1)} %maximum_select_fusion.5), channel_id=1, source_target_pairs={{0,64},{4,68},{8,72},{12,76},{16,80},{20,84},{24,88},{28,92},{32,9... | collective-permute-start | bytes 1572872 | tf_op jit(solution)/shard_map/ppermute | solution.py:8
  380.6 52.9 %collective-permute-start.20 = (bf16[64,64,128]{2,1,0:T(8,128)(2,1)S(1)}, bf16[64,64,128]{2,1,0:T(8,128)(2,1)}, u32[]{:S(2)}, u32[]{:S(2)}) collective-permute-start(bf16[64,64,128]{2,1,0:T(8,128)(2,1)S(1)} %maximum_select_fusion.2), channel_id=1, source_target_pairs={{0,128},{4,132},{8,136},{12,140},{16,144},{20,148},{24,152},{28,15... | collective-permute-start | bytes 3145736 | tf_op jit(solution)/shard_map/ppermute | solution.py:8
  387.9 0.6 copy-start.1
Sparse Core Ops, SparseCore 0:
  15.2 44.5 all-reduce.6
  69.6 45.1 all-reduce.8
  130.0 46.3 all-reduce.10
  197.0 47.4 all-reduce.12
  290.9 45.8 all-reduce.14
  437.8 42.0 all-reduce.16
where the time goes:
time: 490 us; the launch traced here: 489 us
  waiting for transfers between devices  396 us (81%)
  starting transfers between devices  51.2 us (10%)
  matrix products  16.3 us (3%)
  between operations  13.7 us (3%)
  local copies, waits for them, and re-layouts  7.1 us (1%)
    psum x6, waiting for transfers between devices, on_device(): total = lax.psum(partial_value, 'col')  271 us
    ppermute x21, waiting for transfers between devices, partner(): lax.ppermute(x, axis, [(i, i ^ 1 << stride) for i in range(lax.axis_size(...  125 us
    ppermute x21, starting transfers between devices, partner(): lax.ppermute(x, axis, [(i, i ^ 1 << stride) for i in range(lax.axis_size(...  51 us
  transfers between devices with their start and end apart: 27, of which 26 were waited for; matrix products, arithmetic and copies ran while one was open for 1% of the time, Pallas kernels for 0%

commit v1 on v0

v1 whole, which is shorter than its diff:
```python
import functools

import jax
import jax.numpy as jnp
from jax import lax
from jax.experimental import pallas as pl
from jax.experimental.pallas import tpu as pltpu
from jax.sharding import PartitionSpec as P

MESH = pl.DeviceIdType.MESH
LOCAL_LEVELS = 3
SPLIT_ABOVE = 4
FEED = (0, 1, 1, 1, 1, 1, 2, 0, 4, 0, 4, 0)


def nt_dot(a, b, precision=None):
    return lax.dot_general(
        a, b, (((1,), (1,)), ((), ())), precision=precision, preferred_element_type=jnp.float32
    )


def inverse_dot(resid, inverse):
    return nt_dot(resid, inverse, lax.Precision.HIGHEST)


def kernel(depth, near, cols, rhs, inv, low, idx, out, *scratch):
    s = dict(zip(scratch_names(depth, near), scratch, strict=True))
    row, col = lax.axis_index("row"), lax.axis_index("col")
    share = rhs.shape[2] // cols
    slots = low.shape[2]
    far = depth - near
    core = row % 2
    mate = row + 1 - 2 * core
    rhs0, rhsq, invv, lowa, lows, idxv, idxs, idxo, pairs = (
        s[k] for k in ("rhs0", "rhsq", "invv", "lowa", "lows", "idxv", "idxs", "idxo", "pairs")
    )

    load = s["load_sem"]
    quarter = pl.ds(pl.multiple_of(col * share, share), share)
    load_rhs0 = pltpu.make_async_copy(rhs.at[0], rhs0, load.at[0])
    load_inv0 = pltpu.make_async_copy(inv.at[0], invv.at[0], load.at[1])
    load_idx = pltpu.make_async_copy(idx, idxv.at[col], load.at[2])
    load_own = pltpu.make_async_copy(idx, idxo, load.at[3])
    load_low = pltpu.make_async_copy(low.at[pl.ds(0, near)], lowa, load.at[4])
    load_inv = pltpu.make_async_copy(
        inv.at[pl.ds(1, depth)], invv.at[pl.ds(1, depth)], load.at[5]
    )
    load_rhs = pltpu.make_async_copy(
        rhs.at[pl.ds(1, depth), :, quarter], rhsq, load.at[6]
    )
    load_far = [
        pltpu.make_async_copy(low.at[near + i], lows.at[i, col], s["own_sem"].at[i])
        for i in range(far)
    ]
    for copy in (load_rhs0, load_inv0, load_idx, load_own, load_low, load_inv, load_rhs, *load_far):
        copy.start()

    barrier = pltpu.get_barrier_semaphore()
    greeted = 0

    def greet(target):
        pl.semaphore_signal(barrier, 1, device_id=target, device_id_type=MESH)

    for bit in reversed(range(1, depth)):
        n = 2 << bit
        greet((row - row % n + (row % n + n // 2) % n, col))
        greeted += 1
    for e in (2, 1, 3, 0):
        greet((mate, (col + e) % cols))
        greeted += 1
        if e:
            greet((row, (col + e) % cols))
            greeted += 1

    load_rhs0.wait()
    load_inv0.wait()
    for n in range(2):
        x0 = inverse_dot(rhs0[n], invv[0, n])
        pairs[core * 2 + n] = x0.astype(jnp.bfloat16)
        rhs0[n] = x0
    pl.semaphore_wait(barrier, greeted)

    def send(src, dst, send_sem, recv_sem, target):
        pltpu.make_async_remote_copy(
            src_ref=src, dst_ref=dst, send_sem=send_sem, recv_sem=recv_sem,
            device_id=target, device_id_type=MESH,
        ).start()

    def wait_bytes(ref, sem):
        pltpu.make_async_copy(ref, ref, sem).wait()

    pieces = [(i, n, half) for i in range(far) for n in range(2) for half in range(2)]

    def feed(count):
        for i, n, half in pieces[:count]:
            at = pl.ds(half * (slots // 2), slots // 2)
            for e in (2, 1, 3):
                send(low.at[near + i, n, at], lows.at[i, col, n, at],
                     s["low_send"].at[i], s["low_recv"].at[i], (row, (col + e) % cols))
        del pieces[:count]

    mine = pairs.at[pl.ds(core * 2, 2)]
    send(mine, mine, s["gather_send"].at[0], s["gather_recv"].at[0], (mate, col))
    load_idx.wait()
    for e in (2, 1, 3):
        send(idxv.at[col], idxv.at[col], s["idx_send"], s["idx_recv"], (row, (col + e) % cols))
    feed(FEED[0])
    for n in range(2):
        out[0, n] = rhs0[n, quarter]
    load_own.wait()
    load_low.wait()
    load_inv.wait()
    load_rhs.wait()

    for level in range(1, depth + 1):
        n_rows = 1 << level
        gather = pairs if level == 1 else s[f"gather{level}"]
        recv = s["gather_recv"].at[level - 1]
        split = is_split(level, near)
        if level == 1:
            wait_bytes(gather.at[pl.ds(0, 2)], recv)
        elif level <= near:
            flat = gather.reshape(cols * 2 * n_rows, share, gather.shape[-1])
            wait_bytes(flat.at[pl.ds(0, 2 * (n_rows * cols - 1))], recv)
        elif split:
            wait_bytes(gather.at[0, pl.ds(0, n_rows // 2 - 1)], recv)
            half = gather.at[core]
            sems = s["mate_send"].at[level - 1], s["mate_recv"].at[level - 1]
            send(half, half, *sems, (mate, col))
        else:
            wait_bytes(gather.at[pl.ds(0, 2 * (n_rows - 1))], recv)
        if level <= near:
            part, got = s["part"], s["got"]
            for n in range(2):
                picked, blocks = [], []
                for k in range(slots):
                    at = idxo[n, k, level - 1]
                    one = gather[at] if level == 1 else gather[:, at].reshape(cols * share, -1)
                    picked.append(one)
                    blocks.append(lowa[level - 1, n, k])
                partial = nt_dot(jnp.concatenate(picked, 1), jnp.concatenate(blocks, 1))
                part[level - 1, :, n] = partial.reshape(cols, share, -1)
            for e in (2, 1, 3):
                to = (col + e) % cols
                send(part.at[level - 1, to], got.at[level - 1, e - 1], s["part_send"].at[level - 1],
                     s["part_recv"].at[level - 1], (row, to))
            feed(FEED[2 * level - 1])
            wait_bytes(got.at[level - 1], s["part_recv"].at[level - 1])
            total = (part[level - 1, col] + got[level - 1, 0]) + (got[level - 1, 1] + got[level - 1, 2])
        else:
            i = level - near - 1
            if i == 0:
                wait_bytes(idxv.at[pl.ds(0, cols - 1)], s["idx_recv"])
                to_scalar = pltpu.make_async_copy(idxv, idxs, load.at[7])
                to_scalar.start()
                to_scalar.wait()
            load_far[i].wait()
            wait_bytes(lows.at[i, pl.ds(0, cols - 1)], s["low_recv"].at[i])
            if split:
                wait_bytes(gather.at[0], s["mate_recv"].at[level - 1])
            sums = []
            for n in range(2):
                picked, blocks = [], []
                for e in range(cols):
                    for k in range(slots):
                        at = idxs[e, n, k, level - 1]
                        picked.append(gather[(at >> 1) & 1, at >> 2, at & 1] if split else gather[at])
                        blocks.append(lows[i, e, n, k])
                sums.append(nt_dot(jnp.concatenate(picked, 1), jnp.concatenate(blocks, 1)))
            total = jnp.stack(sums, 0)
        x = [inverse_dot(rhsq[level - 1, n] - total[n], invv[level, n]) for n in range(2)]
        if level < depth:
            later = 2 * n_rows
            base, here = row - row % later, row % later
            onward = s[f"gather{level + 1}"]
            sems = s["gather_send"].at[level], s["gather_recv"].at[level]
            if level < near:
                mine = onward.at[col, pl.ds(2 * here, 2)]

                def to_rows(d, _):
                    for e in (2, 1, 3, 0):
                        send(mine, mine, *sems, (base + (here + d) % later, (col + e) % cols))
                    return _

            elif is_split(level + 1, near):
                mine = onward.at[core, here // 2]

                def to_rows(d, _):
                    chip = (here // 2 + d) % (later // 2)
                    send(mine, mine, *sems, (base + chip * 2 + core, col))
                    return _

            else:
                mine = onward.at[pl.ds(2 * here, 2)]

                def to_rows(d, _):
                    send(mine, mine, *sems, (base + (here + d) % later, col))
                    return _

            for n in range(2):
                mine[n] = x[n].astype(jnp.bfloat16)
            if level < near:
                for e in (2, 1, 3):
                    send(mine, mine, *sems, (row, (col + e) % cols))
            lax.fori_loop(1, later // 2 if is_split(level + 1, near) else later, to_rows, 0)
            due = sum(i < level + 1 - near for i, _, _ in pieces)
            feed(max(FEED[2 * level], due))
        for n in range(2):
            out[level, n] = x[n]

    wait_bytes(idxv.at[pl.ds(0, cols - 1)], s["idx_send"])
    wait_bytes(pairs.at[pl.ds(0, 2)], s["gather_send"].at[0])
    for level in range(1, depth + 1):
        gather = None if level == 1 else s[f"gather{level}"]
        sent = s["gather_send"].at[level - 1]
        if 1 < level <= near:
            flat = gather.reshape(cols * (2 << level), share, gather.shape[-1])
            wait_bytes(flat.at[pl.ds(0, 2 * ((cols << level) - 1))], sent)
        elif is_split(level, near):
            wait_bytes(gather.at[0, pl.ds(0, (1 << level) // 2 - 1)], sent)
            wait_bytes(gather.at[0], s["mate_send"].at[level - 1])
        elif level > near:
            wait_bytes(gather.at[pl.ds(0, 2 * ((1 << level) - 1))], sent)
        if level <= near:
            wait_bytes(s["got"].at[level - 1], s["part_send"].at[level - 1])
        else:
            wait_bytes(lows.at[level - near - 1, pl.ds(0, cols - 1)], s["low_send"].at[level - near - 1])


def is_split(level, near):
    return level > max(near, SPLIT_ABOVE)


NAMES = (
    "rhs0", "rhsq", "invv", "lowa", "lows", "idxv", "idxs", "idxo", "pairs", "part", "got",
    "load_sem", "own_sem", "idx_send", "idx_recv", "gather_send", "gather_recv",
    "part_send", "part_recv", "low_send", "low_recv", "mate_send", "mate_recv",
)


def scratch_names(depth, near):
    return [*NAMES, *(f"gather{level}" for level in range(2, depth + 1))]


def on_device(depth, near, cols, rhs, inv, low, idx):
    levels, two, wide, block = rhs.shape
    share = wide // cols
    slots = low.shape[2]
    far = depth - near
    idx = idx.transpose(1, 2, 0)
    dma = pltpu.SemaphoreType.DMA
    f32, bf16 = jnp.float32, jnp.bfloat16
    scratch = [
        pltpu.VMEM((two, wide, block), f32),
        pltpu.VMEM((depth, two, share, block), f32),
        pltpu.VMEM((levels, two, block, block), f32),
        pltpu.VMEM((near, two, slots, block, block), bf16),
        pltpu.VMEM((far, cols, two, slots, block, block), bf16),
        pltpu.VMEM((cols, *idx.shape), jnp.int32),
        pltpu.SMEM((cols, *idx.shape), jnp.int32),
        pltpu.SMEM(idx.shape, jnp.int32),
        pltpu.VMEM((2 * two, wide, block), bf16),
        pltpu.VMEM((near, cols, two, share, block), f32),
        pltpu.VMEM((near, cols - 1, two, share, block), f32),
        dma((8,)), dma((far,)), dma, dma,
        dma((depth,)), dma((depth,)), dma((near,)), dma((near,)), dma((far,)), dma((far,)),
        dma((depth,)), dma((depth,)),
    ]
    for level in range(2, depth + 1):
        rows = two << level
        lead = (cols, rows) if level <= near else (2, rows // 4, 2) if is_split(level, near) else (rows,)
        scratch.append(pltpu.VMEM((*lead, share, block), bf16))
    stay = pl.BlockSpec(memory_space=pltpu.HBM)
    return pl.pallas_call(
        functools.partial(kernel, depth, near, cols),
        out_shape=jax.ShapeDtypeStruct((levels, two, share, block), f32),
        in_specs=[stay] * 4,
        out_specs=pl.BlockSpec(memory_space=pltpu.VMEM),
        scratch_shapes=scratch,
        compiler_params=pltpu.CompilerParams(
            collective_id=0, has_side_effects=True, vmem_limit_bytes=61 << 20
        ),
    )(rhs, inv, low, idx)


def solution(mesh):
    depth = mesh.shape["row"].bit_length() - 1
    near = min(LOCAL_LEVELS, depth - 1)
    return jax.shard_map(
        functools.partial(on_device, depth, near, mesh.shape["col"]),
        mesh=mesh,
        in_specs=(
            P(None, "row", None, None),
            P(None, "row", None, None),
            P(None, "row", "col", None, None),
            P(None, "row", "col"),
        ),
        out_specs=P(None, "row", "col", None),
        check_vma=False,
    )
```

time: 490 us -> 63.6 us (0.13)
  waiting for transfers between devices: 396 us -> 0 us
  Pallas kernels: 0 us -> 61.9 us
  starting transfers between devices: 51.2 us -> 0 us
  matrix products: 16.3 us -> 0 us
  between operations: 13.7 us -> 0.01 us
  local copies, waits for them, and re-layouts: 7.1 us -> 1.55 us
    psum x6 -> x0, waiting for transfers between devices: 271 us -> none  [on_device(): total = lax.psum(partial_value, 'col')]
    ppermute x21 -> x0, waiting for transfers between devices: 125 us -> none  [partner(): lax.ppermute(x, axis, [(i, i ^ 1 << stride) for i in range(lax.axis_size(...]
    pallas_call x0 -> x1, Pallas kernels: none -> 61.9 us  [on_device(): pl.pallas_call(functools.partial(kernel, depth, near, cols), out_shape=ja...]
    ppermute x21 -> x0, starting transfers between devices: 51 us -> none  [partner(): lax.ppermute(x, axis, [(i, i ^ 1 << stride) for i in range(lax.axis_size(...]
    dot_general x13 -> x0, matrix products: 16.3 us -> none  [the longest x7 9.41 us: apply_inverse(): jnp.einsum('nsq,nrq->nsr', resid, inverse, precision=lax.Precision.HIGHEST)]
  transfers between devices with their start and end apart: 27 -> 0, of which waited for: 26 -> 0; matrix products, arithmetic and copies ran while one was open for 1% -> 0% of each run, Pallas kernels for 0% -> 0%
where the time goes in v1:
time: 63.6 us; the launch traced here: 63.5 us
  Pallas kernels  61.9 us (97%)
  local copies, waits for them, and re-layouts  1.55 us (2%)
    pallas_call x1, Pallas kernels, on_device(): pl.pallas_call(functools.partial(kernel, depth, near, cols), out_shape=ja...  61.9 us
    unnamed x1, local copies, waits for them, and re-layouts  1.55 us

profile of v1, /device:TPU:1, one launch (start us, length us, event | category | flops | bytes accessed | tf_op | source)
XLA Modules:
  0.0 63.5 jit_solution(2620008180721380494)
XLA Ops:
  0.0 61.9 %shard_map.46 = f32[7,2,16,128]{3,2,1,0:T(8,128)} custom-call(f32[7,2,64,128]{3,2,1,0:T(8,128)} %rhs.1, f32[7,2,128,128]{3,2,1,0:T(8,128)} %inv.1, bf16[6,2,4,128,128]{4,3,2,1,0:T(8,128)(2,1)} %low.1, s32[2,4,6]{2,1,0:T(4,128)} %bitcast.1), custom_call_target="tpu_custom_call" | custom-call | tf_op jit(solution)/shard_map/pallas_call | solution.py:274
  61.9 1.6 %copy.6 = f32[7,2,16,128]{3,2,1,0:T(8,128)} copy(f32[7,2,16,128]{3,2,1,0:T(8,128)} %shard_map.46) | data formatting | bytes 229376

commit v2 on v1

v2 whole, which is shorter than its diff:
```python
import functools

import jax
import jax.numpy as jnp
from jax import lax
from jax.experimental import pallas as pl
from jax.experimental.pallas import tpu as pltpu
from jax.sharding import PartitionSpec as P

MESH = pl.DeviceIdType.MESH
ROW_LEVELS = 3
SPLIT_ABOVE = 4
FEED = (0, 0, 2, 2, 2, 3, 3)


def nt_dot(a, b, precision=None):
    return lax.dot_general(
        a, b, (((1,), (1,)), ((), ())), precision=precision, preferred_element_type=jnp.float32
    )


def inverse_dot(resid, inverse):
    return nt_dot(resid, inverse, lax.Precision.HIGHEST)


def kernel(depth, mid, cols, rhs, inv, low, idx, out, *scratch):
    s = dict(zip(scratch_names(depth), scratch, strict=True))
    row, col = lax.axis_index("row"), lax.axis_index("col")
    share = rhs.shape[2] // cols
    slots = low.shape[2]
    far, chips = depth - mid, mid - 1
    core, chip = row % 2, row // 2
    mate = row + 1 - 2 * core
    home, place = col // 2, col % 2
    at_home = core == home
    rhs0, rhsq, invv, lowa, lows, lowc, idxv, idxs, idxo, pairs = (
        s[k]
        for k in ("rhs0", "rhsq", "invv", "lowa", "lows", "lowc", "idxv", "idxs", "idxo", "pairs")
    )

    def send(src, dst, send_sem, recv_sem, target):
        pltpu.make_async_remote_copy(
            src_ref=src, dst_ref=dst, send_sem=send_sem, recv_sem=recv_sem,
            device_id=target, device_id_type=MESH,
        ).start()

    def hand(here, src, dst, send_sem, recv_sem, target):
        @pl.when(here)
        def _():
            pltpu.make_async_copy(src, dst, recv_sem).start()

        @pl.when(jnp.logical_not(here))
        def _():
            send(src, dst, send_sem, recv_sem, target)

    def wait_bytes(ref, sem):
        pltpu.make_async_copy(ref, ref, sem).wait()

    def wait_if_away(ref, sem):
        @pl.when(jnp.logical_not(at_home))
        def _():
            wait_bytes(ref, sem)

    load = s["load_sem"]
    quarter = pl.ds(pl.multiple_of(col * share, share), share)
    load_rhs0 = pltpu.make_async_copy(rhs.at[0], rhs0, load.at[0])
    load_inv0 = pltpu.make_async_copy(inv.at[0], invv.at[0], load.at[1])
    load_idx = pltpu.make_async_copy(idx, idxv.at[core, col], load.at[2])
    load_own = pltpu.make_async_copy(idx, idxo, load.at[3])
    load_low = pltpu.make_async_copy(low.at[0], lowa, load.at[4])
    load_inv = pltpu.make_async_copy(
        inv.at[pl.ds(1, depth)], invv.at[pl.ds(1, depth)], load.at[5]
    )
    load_rhs = pltpu.make_async_copy(
        rhs.at[pl.ds(1, depth), :, quarter], rhsq, load.at[6]
    )
    load_far = [
        pltpu.make_async_copy(low.at[mid + i], lows.at[i, col], s["own_sem"].at[i])
        for i in range(far)
    ]
    for copy in (load_rhs0, load_inv0, load_idx, load_own, load_low, load_inv, load_rhs, *load_far):
        copy.start()

    barrier = pltpu.get_barrier_semaphore()
    greeted = 0

    def greet(target):
        pl.semaphore_signal(barrier, 1, device_id=target, device_id_type=MESH)

    for bit in reversed(range(1, depth)):
        n = 2 << bit
        greet((row - row % n + (row % n + n // 2) % n, col))
        greeted += 1
    for e in (2, 1, 3, 0):
        greet((mate, (col + e) % cols))
        greeted += 1
        if e:
            greet((row, (col + e) % cols))
            greeted += 1

    load_rhs0.wait()
    load_inv0.wait()
    for n in range(2):
        x0 = inverse_dot(rhs0[n], invv[0, n])
        pairs[core * 2 + n] = x0.astype(jnp.bfloat16)
        rhs0[n] = x0
    pl.semaphore_wait(barrier, greeted)

    mine = pairs.at[pl.ds(core * 2, 2)]
    send(mine, mine, s["gather_send"].at[0], s["gather_recv"].at[0], (mate, col))

    def feed_row(j):
        for n in range(2):
            to = core * 2 + n
            for t in range(2):
                at = pl.ds(t * (slots // 2), slots // 2)
                hand((to == col) & (core == t), low.at[j + 1, n, at], lowc.at[j, col, at],
                     s["row_send"].at[j], s["row_recv"].at[j], (chip * 2 + t, to))

    pieces = [(i, n, half) for i in range(far) for n in range(2) for half in range(2)]

    def feed(count):
        for i, n, half in pieces[:count]:
            at = pl.ds(half * (slots // 2), slots // 2)
            for e in (2, 1, 3):
                send(low.at[mid + i, n, at], lows.at[i, col, n, at],
                     s["low_send"].at[i], s["low_recv"].at[i], (row, (col + e) % cols))
        del pieces[:count]

    feed_row(0)
    load_idx.wait()
    for e in (2, 1, 3, 0):
        for target in (row, mate):
            if e or target is mate:
                send(idxv.at[core, col], idxv.at[core, col], s["idx_send"], s["idx_recv"],
                     (target, (col + e) % cols))

    @pl.when(at_home)
    def _():
        for j in range(chips):
            for target, half in ((row, core), (mate, 1 - core)):
                at = pl.ds(pl.multiple_of(half * 2 * share, 2 * share), 2 * share)
                for src, dst, k in (
                    (rhs.at[j + 2, place, at], s["rhsc"].at[j], 0),
                    (inv.at[j + 2, place], s["invc"].at[j], 1),
                ):
                    if target is row:
                        pltpu.make_async_copy(src, dst, s["side_recv"].at[j, k]).start()
                    else:
                        send(src, dst, s["side_send"].at[j, k], s["side_recv"].at[j, k], (mate, col))

    feed(FEED[0])
    for n in range(2):
        out[0, n] = rhs0[n, quarter]
    load_own.wait()
    load_low.wait()
    load_inv.wait()
    load_rhs.wait()

    for level in range(1, depth + 1):
        n_rows = 1 << level
        gather = pairs if level == 1 else s[f"gather{level}"]
        recv = s["gather_recv"].at[level - 1]
        split = is_split(level, mid)
        if level == 1:
            wait_bytes(gather.at[pl.ds(0, 2)], recv)
        elif level <= mid + 1:
            wait_bytes(gather, recv)
        elif split:
            wait_bytes(gather.at[0, pl.ds(0, n_rows // 2 - 1)], recv)
            half = gather.at[core]
            sems = s["mate_send"].at[level - 1], s["mate_recv"].at[level - 1]
            send(half, half, *sems, (mate, col))
        else:
            wait_bytes(gather.at[pl.ds(0, 2 * (n_rows - 1))], recv)
        if level == 1:
            part, got = s["part"], s["got"]
            for n in range(2):
                picked, blocks = [], []
                for k in range(slots):
                    picked.append(gather[idxo[n, k, 0]])
                    blocks.append(lowa[n, k])
                partial = nt_dot(jnp.concatenate(picked, 1), jnp.concatenate(blocks, 1))
                part[:, n] = partial.reshape(cols, share, -1)
            for e in (2, 1, 3):
                to = (col + e) % cols
                send(part.at[to], got.at[e - 1], s["part_send"], s["part_recv"], (row, to))
            for j in range(1, chips):
                feed_row(j)
            feed(FEED[1])
            wait_bytes(idxv.reshape(2 * cols, *idx.shape).at[pl.ds(0, 2 * cols - 1)], s["idx_recv"])
            to_scalar = pltpu.make_async_copy(idxv, idxs, load.at[7])
            to_scalar.start()
            wait_bytes(got, s["part_recv"])
            total = (part[col] + got[0]) + (got[1] + got[2])
        elif level <= mid:
            j = level - 2
            wait_bytes(s["rhsc"].at[j], s["side_recv"].at[j, 0])
            wait_bytes(s["invc"].at[j], s["side_recv"].at[j, 1])
            wait_bytes(lowc.at[j, :, pl.ds(0, slots // 2)], s["pass_recv"].at[j])
            picked, blocks = [], []
            for e in range(cols):
                for k in range(slots):
                    at = idxs[home, e, place, k, level - 1]
                    picked.append(gather[at].reshape(2 * share, -1))
                    blocks.append(lowc[j, e, k])
            total = nt_dot(jnp.concatenate(picked, 1), jnp.concatenate(blocks, 1))
        else:
            i = level - mid - 1
            load_far[i].wait()
            wait_bytes(lows.at[i, pl.ds(0, cols - 1)], s["low_recv"].at[i])
            if split:
                wait_bytes(gather.at[0], s["mate_recv"].at[level - 1])
            sums = []
            for n in range(2):
                picked, blocks = [], []
                for e in range(cols):
                    for k in range(slots):
                        at = idxs[core, e, n, k, level - 1]
                        picked.append(gather[(at >> 1) & 1, at >> 2, at & 1] if split else gather[at])
                        blocks.append(lows[i, e, n, k])
                sums.append(nt_dot(jnp.concatenate(picked, 1), jnp.concatenate(blocks, 1)))
            total = jnp.stack(sums, 0)
        in_row = 1 < level <= mid
        if in_row:
            x = inverse_dot(s["rhsc"][level - 2] - total, s["invc"][level - 2])
            x = [x[q * share : (q + 1) * share] for q in range(2)]
        else:
            x = [inverse_dot(rhsq[level - 1, n] - total[n], invv[level, n]) for n in range(2)]
        if level < depth:
            later = 2 * n_rows
            base, here = row - row % later, row % later
            here_chip = here // 2
            onward = s[f"gather{level + 1}"]
            sems = s["gather_send"].at[level], s["gather_recv"].at[level]
            count = later // 2
            if level <= mid:
                mine = s["held"].at[level - 1]
                for n in range(2):
                    mine[n] = x[n].astype(jnp.bfloat16)
            if level == 1:
                slot = onward.at[pl.ds(here_chip * 4 + core * 2, 2), place]

                def to_chips(d, _):
                    target = base + (here_chip + d) % count * 2 + home
                    for e in (2, 1, 3, 0):
                        send(mine, slot, *sems, (target, (col + e) % cols))
                    return _

                for e in (2, 1, 3):
                    send(mine, slot, *sems, (chip * 2 + home, (col + e) % cols))
                hand(at_home, mine, slot, *sems, (mate, col))
            elif level < mid:
                slot = onward.at[here_chip * 4 + col]

                def to_chips(d, _):
                    target = base + (here_chip + d) % count * 2 + core
                    for e in (2, 1, 3, 0):
                        send(mine, slot, *sems, (target, (col + e) % cols))
                    return _

                for e in (2, 1, 3):
                    send(mine, slot, *sems, (row, (col + e) % cols))
                pltpu.make_async_copy(mine, slot, sems[1]).start()
            elif level == mid:
                slot = onward.at[here_chip * 4 + col]

                def to_chips(d, _):
                    target = base + (here_chip + d) % count * 2
                    for t in range(2):
                        for q in range(2):
                            send(mine.at[q], slot, *sems, (target + t, core * 2 + q))
                    return _

                for q in range(2):
                    to = core * 2 + q
                    send(mine.at[q], slot, *sems, (mate, to))
                    hand(to == col, mine.at[q], slot, *sems, (row, to))
            elif is_split(level + 1, mid):
                mine = onward.at[core, here_chip]

                def to_chips(d, _):
                    send(mine, mine, *sems, (base + (here_chip + d) % count * 2 + core, col))
                    return _

            else:
                mine = onward.at[pl.ds(2 * here, 2)]
                count = later

                def to_chips(d, _):
                    send(mine, mine, *sems, (base + (here + d) % later, col))
                    return _

            if level > mid:
                for n in range(2):
                    mine[n] = x[n].astype(jnp.bfloat16)
            lax.fori_loop(1, count, to_chips, 0)
            if level == 1:
                to_scalar.wait()
            if level < mid:
                j = level - 1
                half = pl.ds(core * (slots // 2), slots // 2)
                wait_bytes(lowc.at[j, :, pl.ds(0, slots // 2)], s["row_recv"].at[j])
                send(lowc.at[j, :, half], lowc.at[j, :, half], s["pass_send"].at[j], s["pass_recv"].at[j],
                     (mate, col))
            due = sum(i < level + 1 - mid for i, _, _ in pieces)
            feed(max(FEED[level + 1], due))
        if in_row:
            j = level - 2
            for q in range(2):
                s["wide"][j, q] = x[q]
                to = core * 2 + q
                hand((to == col) & at_home, s["wide"].at[j, q], s["owned"].at[j, place],
                     s["own_send"].at[j], s["own_recv"].at[j], (chip * 2 + home, to))
        else:
            for n in range(2):
                out[level, n] = x[n]

    for j in range(chips):
        wait_bytes(s["owned"].at[j], s["own_recv"].at[j])
        out[j + 2] = s["owned"][j]

    wait_bytes(idxv.reshape(2 * cols, *idx.shape).at[pl.ds(0, 2 * cols - 1)], s["idx_send"])
    wait_bytes(pairs.at[pl.ds(0, 2)], s["gather_send"].at[0])
    wait_bytes(s["got"], s["part_send"])
    for j in range(chips):
        wait_bytes(lowc.at[j, pl.ds(0, cols - 1), pl.ds(0, slots // 2)], s["row_send"].at[j])
        wait_if_away(lowc.at[j, 0, pl.ds(0, slots // 2)], s["row_send"].at[j])
        wait_bytes(lowc.at[j, :, pl.ds(0, slots // 2)], s["pass_send"].at[j])
        wait_bytes(s["wide"].at[j, 0], s["own_send"].at[j])
        wait_if_away(s["wide"].at[j, 0], s["own_send"].at[j])

    @pl.when(at_home)
    def _():
        for j in range(chips):
            wait_bytes(s["rhsc"].at[j], s["side_send"].at[j, 0])
            wait_bytes(s["invc"].at[j], s["side_send"].at[j, 1])

    for level in range(2, depth + 1):
        gather, sent = s[f"gather{level}"], s["gather_send"].at[level - 1]
        n_rows = 1 << level
        if level == 2 or level == mid + 1:
            one = gather.at[pl.ds(0, 2), 0] if level == 2 else gather.at[0]
            rest = gather.at[pl.ds(0, 7)] if level == 2 else gather.at[pl.ds(0, 2 * n_rows - 1)]
            wait_bytes(rest, sent)
            wait_if_away(one, sent)
        elif level <= mid:
            wait_bytes(gather.at[pl.ds(0, 2 * n_rows - 1)], sent)
        elif is_split(level, mid):
            wait_bytes(gather.at[0, pl.ds(0, n_rows // 2 - 1)], sent)
            wait_bytes(gather.at[0], s["mate_send"].at[level - 1])
        else:
            wait_bytes(gather.at[pl.ds(0, 2 * (n_rows - 1))], sent)
    for i in range(far):
        wait_bytes(lows.at[i, pl.ds(0, cols - 1)], s["low_send"].at[i])


def is_split(level, mid):
    return level > max(mid + 1, SPLIT_ABOVE)


NAMES = (
    "rhs0", "rhsq", "invv", "lowa", "lows", "lowc", "idxv", "idxs", "idxo", "pairs", "part", "got",
    "rhsc", "invc", "held", "wide", "owned", "load_sem", "own_sem", "idx_send", "idx_recv",
    "gather_send", "gather_recv", "part_send", "part_recv", "low_send", "low_recv", "mate_send",
    "mate_recv", "row_send", "row_recv", "pass_send", "pass_recv", "side_send", "side_recv",
    "own_send", "own_recv",
)


def scratch_names(depth):
    return [*NAMES, *(f"gather{level}" for level in range(2, depth + 1))]


def on_device(depth, mid, cols, rhs, inv, low, idx):
    levels, two, wide, block = rhs.shape
    share = wide // cols
    slots = low.shape[2]
    far, chips = depth - mid, mid - 1
    idx = idx.transpose(1, 2, 0)
    dma = pltpu.SemaphoreType.DMA
    f32, bf16 = jnp.float32, jnp.bfloat16
    scratch = [
        pltpu.VMEM((two, wide, block), f32),
        pltpu.VMEM((depth, two, share, block), f32),
        pltpu.VMEM((levels, two, block, block), f32),
        pltpu.VMEM((two, slots, block, block), bf16),
        pltpu.VMEM((far, cols, two, slots, block, block), bf16),
        pltpu.VMEM((chips, cols, slots, block, block), bf16),
        pltpu.VMEM((2, cols, *idx.shape), jnp.int32),
        pltpu.SMEM((2, cols, *idx.shape), jnp.int32),
        pltpu.SMEM(idx.shape, jnp.int32),
        pltpu.VMEM((2 * two, wide, block), bf16),
        pltpu.VMEM((cols, two, share, block), f32),
        pltpu.VMEM((cols - 1, two, share, block), f32),
        pltpu.VMEM((chips, 2 * share, block), f32),
        pltpu.VMEM((chips, block, block), f32),
        pltpu.VMEM((mid, 2, share, block), bf16),
        pltpu.VMEM((chips, 2, share, block), f32),
        pltpu.VMEM((chips, two, share, block), f32),
        dma((8,)), dma((far,)), dma, dma,
        dma((depth,)), dma((depth,)), dma, dma, dma((far,)), dma((far,)), dma((depth,)),
        dma((depth,)), dma((chips,)), dma((chips,)), dma((chips,)), dma((chips,)), dma((chips, 2)), dma((chips, 2)),
        dma((chips,)), dma((chips,)),
    ]
    for level in range(2, depth + 1):
        rows = two << level
        lead = (rows, 2) if level <= mid else (2, rows // 4, 2) if is_split(level, mid) else (rows,)
        scratch.append(pltpu.VMEM((*lead, share, block), bf16))
    stay = pl.BlockSpec(memory_space=pltpu.HBM)
    return pl.pallas_call(
        functools.partial(kernel, depth, mid, cols),
        out_shape=jax.ShapeDtypeStruct((levels, two, share, block), f32),
        in_specs=[stay] * 4,
        out_specs=pl.BlockSpec(memory_space=pltpu.VMEM),
        scratch_shapes=scratch,
        compiler_params=pltpu.CompilerParams(
            collective_id=0, has_side_effects=True, vmem_limit_bytes=61 << 20
        ),
    )(rhs, inv, low, idx)


def solution(mesh):
    depth = mesh.shape["row"].bit_length() - 1
    mid = min(ROW_LEVELS, depth - 1)
    return jax.shard_map(
        functools.partial(on_device, depth, mid, mesh.shape["col"]),
        mesh=mesh,
        in_specs=(
            P(None, "row", None, None),
            P(None, "row", None, None),
            P(None, "row", "col", None, None),
            P(None, "row", "col"),
        ),
        out_specs=P(None, "row", "col", None),
        check_vma=False,
    )
```

time: 63.6 us -> 61.6 us (0.969)
  Pallas kernels: 61.9 us -> 59.9 us
    pallas_call x1, Pallas kernels: 61.9 us -> 59.9 us  [on_device(): pl.pallas_call(functools.partial(kernel, depth, mid, cols), out_shape=jax...]
where the time goes in v2:
time: 61.6 us; the launch traced here: 61.5 us
  Pallas kernels  59.9 us (97%)
  local copies, waits for them, and re-layouts  1.55 us (3%)
    pallas_call x1, Pallas kernels, on_device(): pl.pallas_call(functools.partial(kernel, depth, mid, cols), out_shape=jax...  59.9 us
    unnamed x1, local copies, waits for them, and re-layouts  1.55 us

profile of v2, /device:TPU:1, one launch (start us, length us, event | category | flops | bytes accessed | tf_op | source)
XLA Modules:
  0.0 61.5 jit_solution(4682758485099218274)
XLA Ops:
  0.0 59.9 %shard_map.46 = f32[7,2,16,128]{3,2,1,0:T(8,128)} custom-call(f32[7,2,64,128]{3,2,1,0:T(8,128)} %rhs.1, f32[7,2,128,128]{3,2,1,0:T(8,128)} %inv.1, bf16[6,2,4,128,128]{4,3,2,1,0:T(8,128)(2,1)} %low.1, s32[2,4,6]{2,1,0:T(4,128)} %bitcast.1), custom_call_target="tpu_custom_call" | custom-call | tf_op jit(solution)/shard_map/pallas_call | solution.py:411
  60.0 1.6 %copy.6 = f32[7,2,16,128]{3,2,1,0:T(8,128)} copy(f32[7,2,16,128]{3,2,1,0:T(8,128)} %shard_map.46) | data formatting | bytes 229376

commit v3 on v2

--- a/solution.py
+++ b/solution.py
@@ -10,7 +10,7 @@
 MESH = pl.DeviceIdType.MESH
 ROW_LEVELS = 3
 SPLIT_ABOVE = 4
-FEED = (0, 0, 2, 2, 2, 3, 3)
+FEED = (0, 0, 6, 4, 6, 8, 0)
 
 
 def nt_dot(a, b, precision=None):
@@ -19,8 +19,11 @@
     )
 
 
+PREC = lax.Precision.HIGH
+
+
 def inverse_dot(resid, inverse):
-    return nt_dot(resid, inverse, lax.Precision.HIGHEST)
+    return nt_dot(resid, inverse, PREC)
 
 
 def kernel(depth, mid, cols, rhs, inv, low, idx, out, *scratch):
@@ -117,15 +120,28 @@
                 hand((to == col) & (core == t), low.at[j + 1, n, at], lowc.at[j, col, at],
                      s["row_send"].at[j], s["row_recv"].at[j], (chip * 2 + t, to))
 
-    pieces = [(i, n, half) for i in range(far) for n in range(2) for half in range(2)]
+    blocks_left = [(i, n, k) for i in range(far) for n in range(2) for k in range(slots)]
+    waves, passed = [], []
+    flat_lows = lows.reshape(far * cols * 2 * slots, *low.shape[3:])
 
     def feed(count):
-        for i, n, half in pieces[:count]:
-            at = pl.ds(half * (slots // 2), slots // 2)
-            for e in (2, 1, 3):
-                send(low.at[mid + i, n, at], lows.at[i, col, n, at],
-                     s["low_send"].at[i], s["low_recv"].at[i], (row, (col + e) % cols))
-        del pieces[:count]
+        if not blocks_left[:count]:
+            return
+        for i, n, k in blocks_left[:count]:
+            for e in (1, cols - 1):
+                send(low.at[mid + i, n, k], lows.at[i, col, n, k],
+                     s["low_send"].at[i], s["wave_recv"].at[len(waves)], (row, (col + e) % cols))
+        waves.append(blocks_left[:count])
+        del blocks_left[:count]
+
+    def pass_on():
+        for wave in range(len(passed), len(waves)):
+            passed.append(waves[wave])
+            wait_bytes(flat_lows.at[pl.ds(0, 2 * len(waves[wave]))], s["wave_recv"].at[wave])
+            for i, n, k in waves[wave]:
+                e = 1 if k % 2 == 0 else cols - 1
+                block = lows.at[i, (col + cols - e) % cols, n, k]
+                send(block, block, s["low_send"].at[i], s["low_recv"].at[i], (row, (col + e) % cols))
 
     feed_row(0)
     load_idx.wait()
@@ -150,8 +166,15 @@
                         send(src, dst, s["side_send"].at[j, k], s["side_recv"].at[j, k], (mate, col))
 
     feed(FEED[0])
+    outv, puts = s["outv"], []
+
+    def put(level, src):
+        puts.append(pltpu.make_async_copy(src, out.at[level], s["put_sem"].at[level]))
+        puts[-1].start()
+
     for n in range(2):
-        out[0, n] = rhs0[n, quarter]
+        outv[0, n] = rhs0[n, quarter]
+    put(0, outv.at[0])
     load_own.wait()
     load_low.wait()
     load_inv.wait()
@@ -208,7 +231,7 @@
         else:
             i = level - mid - 1
             load_far[i].wait()
-            wait_bytes(lows.at[i, pl.ds(0, cols - 1)], s["low_recv"].at[i])
+            wait_bytes(lows.at[i, 0], s["low_recv"].at[i])
             if split:
                 wait_bytes(gather.at[0], s["mate_recv"].at[level - 1])
             sums = []
@@ -303,8 +326,9 @@
                 wait_bytes(lowc.at[j, :, pl.ds(0, slots // 2)], s["row_recv"].at[j])
                 send(lowc.at[j, :, half], lowc.at[j, :, half], s["pass_send"].at[j], s["pass_recv"].at[j],
                      (mate, col))
-            due = sum(i < level + 1 - mid for i, _, _ in pieces)
-            feed(max(FEED[level + 1], due))
+            feed(sum(i < level + 1 - mid for i, _, _ in blocks_left))
+            pass_on()
+            feed(FEED[level + 1])
         if in_row:
             j = level - 2
             for q in range(2):
@@ -314,11 +338,12 @@
                      s["own_send"].at[j], s["own_recv"].at[j], (chip * 2 + home, to))
         else:
             for n in range(2):
-                out[level, n] = x[n]
-
-    for j in range(chips):
-        wait_bytes(s["owned"].at[j], s["own_recv"].at[j])
-        out[j + 2] = s["owned"][j]
+                outv[level, n] = x[n]
+            put(level, outv.at[level])
+        if level == depth - 1:
+            for j in range(chips):
+                wait_bytes(s["owned"].at[j], s["own_recv"].at[j])
+                put(j + 2, s["owned"].at[j])
 
     wait_bytes(idxv.reshape(2 * cols, *idx.shape).at[pl.ds(0, 2 * cols - 1)], s["idx_send"])
     wait_bytes(pairs.at[pl.ds(0, 2)], s["gather_send"].at[0])
@@ -353,6 +378,8 @@
             wait_bytes(gather.at[pl.ds(0, 2 * (n_rows - 1))], sent)
     for i in range(far):
         wait_bytes(lows.at[i, pl.ds(0, cols - 1)], s["low_send"].at[i])
+    for copy in puts:
+        copy.wait()
 
 
 def is_split(level, mid):
@@ -364,7 +391,7 @@
     "rhsc", "invc", "held", "wide", "owned", "load_sem", "own_sem", "idx_send", "idx_recv",
     "gather_send", "gather_recv", "part_send", "part_recv", "low_send", "low_recv", "mate_send",
     "mate_recv", "row_send", "row_recv", "pass_send", "pass_recv", "side_send", "side_recv",
-    "own_send", "own_recv",
+    "own_send", "own_recv", "outv", "put_sem", "wave_recv",
 )
 
 
@@ -401,7 +428,8 @@
         dma((8,)), dma((far,)), dma, dma,
         dma((depth,)), dma((depth,)), dma, dma, dma((far,)), dma((far,)), dma((depth,)),
         dma((depth,)), dma((chips,)), dma((chips,)), dma((chips,)), dma((chips,)), dma((chips, 2)), dma((chips, 2)),
-        dma((chips,)), dma((chips,)),
+        dma((chips,)), dma((chips,)), pltpu.VMEM((levels, two, share, block), f32), dma((levels,)),
+        dma((2 * levels,)),
     ]
     for level in range(2, depth + 1):
         rows = two << level
@@ -412,7 +440,7 @@
         functools.partial(kernel, depth, mid, cols),
         out_shape=jax.ShapeDtypeStruct((levels, two, share, block), f32),
         in_specs=[stay] * 4,
-        out_specs=pl.BlockSpec(memory_space=pltpu.VMEM),
+        out_specs=stay,
         scratch_shapes=scratch,
         compiler_params=pltpu.CompilerParams(
             collective_id=0, has_side_effects=True, vmem_limit_bytes=61 << 20

time: 61.6 us -> 58.9 us (0.956)
  Pallas kernels: 59.9 us -> 57.3 us
    pallas_call x1, Pallas kernels: 59.9 us -> 57.3 us  [on_device(): pl.pallas_call(functools.partial(kernel, depth, mid, cols), out_shape=jax...]
where the time goes in v3:
time: 58.9 us; the launch traced here: 58.8 us
  Pallas kernels  57.3 us (97%)
  local copies, waits for them, and re-layouts  1.55 us (3%)
    pallas_call x1, Pallas kernels, on_device(): pl.pallas_call(functools.partial(kernel, depth, mid, cols), out_shape=jax...  57.3 us
    unnamed x1, local copies, waits for them, and re-layouts  1.55 us

profile of v3, /device:TPU:1, one launch (start us, length us, event | category | flops | bytes accessed | tf_op | source)
XLA Modules:
  0.0 58.8 jit_solution(16806901350771885731)
XLA Ops:
  0.0 57.3 %shard_map.46 = f32[7,2,16,128]{3,2,1,0:T(8,128)} custom-call(f32[7,2,64,128]{3,2,1,0:T(8,128)} %rhs.1, f32[7,2,128,128]{3,2,1,0:T(8,128)} %inv.1, bf16[6,2,4,128,128]{4,3,2,1,0:T(8,128)(2,1)} %low.1, s32[2,4,6]{2,1,0:T(4,128)} %bitcast.1), custom_call_target="tpu_custom_call" | custom-call | tf_op jit(solution)/shard_map/pallas_call | solution.py:439
  57.3 1.6 %copy.6 = f32[7,2,16,128]{3,2,1,0:T(8,128)} copy(f32[7,2,16,128]{3,2,1,0:T(8,128)} %shard_map.46) | data formatting | bytes 229376

commit v4 on v3

--- a/solution.py
+++ b/solution.py
@@ -10,7 +10,7 @@
 MESH = pl.DeviceIdType.MESH
 ROW_LEVELS = 3
 SPLIT_ABOVE = 4
-FEED = (0, 0, 6, 4, 6, 8, 0)
+FEED = (0, 0, 6, 2, 8, 8, 0)
 
 
 def nt_dot(a, b, precision=None):
@@ -19,11 +19,14 @@
     )
 
 
-PREC = lax.Precision.HIGH
+def two_parts(x):
+    high = x.astype(jnp.bfloat16)
+    return high, (x - high.astype(jnp.float32)).astype(jnp.bfloat16)
 
 
 def inverse_dot(resid, inverse):
-    return nt_dot(resid, inverse, PREC)
+    (rh, rl), (ih, il) = two_parts(resid), two_parts(inverse)
+    return nt_dot(jnp.concatenate([rh, rh, rl], 1), jnp.concatenate([ih, il, ih], 1))
 
 
 def kernel(depth, mid, cols, rhs, inv, low, idx, out, *scratch):

time: 58.9 us -> 58.1 us (0.986)
  Pallas kernels: 57.3 us -> 56.4 us
    pallas_call x1, Pallas kernels: 57.3 us -> 56.4 us  [on_device(): pl.pallas_call(functools.partial(kernel, depth, mid, cols), out_shape=jax...]
where the time goes in v4:
time: 58.1 us; the launch traced here: 58 us
  Pallas kernels  56.4 us (97%)
  local copies, waits for them, and re-layouts  1.55 us (3%)
    pallas_call x1, Pallas kernels, on_device(): pl.pallas_call(functools.partial(kernel, depth, mid, cols), out_shape=jax...  56.4 us
    unnamed x1, local copies, waits for them, and re-layouts  1.55 us

profile of v4, /device:TPU:1, one launch (start us, length us, event | category | flops | bytes accessed | tf_op | source)
XLA Modules:
  0.0 58.0 jit_solution(2119223517516325841)
XLA Ops:
  0.0 56.4 %shard_map.46 = f32[7,2,16,128]{3,2,1,0:T(8,128)} custom-call(f32[7,2,64,128]{3,2,1,0:T(8,128)} %rhs.1, f32[7,2,128,128]{3,2,1,0:T(8,128)} %inv.1, bf16[6,2,4,128,128]{4,3,2,1,0:T(8,128)(2,1)} %low.1, s32[2,4,6]{2,1,0:T(4,128)} %bitcast.1), custom_call_target="tpu_custom_call" | custom-call | tf_op jit(solution)/shard_map/pallas_call | solution.py:442
  56.4 1.6 %copy.6 = f32[7,2,16,128]{3,2,1,0:T(8,128)} copy(f32[7,2,16,128]{3,2,1,0:T(8,128)} %shard_map.46) | data formatting | bytes 229376

commit v5 on v4

--- a/solution.py
+++ b/solution.py
@@ -10,7 +10,7 @@
 MESH = pl.DeviceIdType.MESH
 ROW_LEVELS = 3
 SPLIT_ABOVE = 4
-FEED = (0, 0, 6, 2, 8, 8, 0)
+FEED = (0, 0, 7, 1, 8, 8, 0)
 
 
 def nt_dot(a, b, precision=None):
@@ -280,7 +280,8 @@
                 slot = onward.at[here_chip * 4 + col]
 
                 def to_chips(d, _):
-                    target = base + (here_chip + d) % count * 2 + core
+                    away = count // 2 + d // 2 * (1 - 2 * (d % 2))
+                    target = base + (here_chip + away) % count * 2 + core
                     for e in (2, 1, 3, 0):
                         send(mine, slot, *sems, (target, (col + e) % cols))
                     return _
@@ -292,7 +293,8 @@
                 slot = onward.at[here_chip * 4 + col]
 
                 def to_chips(d, _):
-                    target = base + (here_chip + d) % count * 2
+                    away = count // 2 + d // 2 * (1 - 2 * (d % 2))
+                    target = base + (here_chip + away) % count * 2
                     for t in range(2):
                         for q in range(2):
                             send(mine.at[q], slot, *sems, (target + t, core * 2 + q))
@@ -306,7 +308,8 @@
                 mine = onward.at[core, here_chip]
 
                 def to_chips(d, _):
-                    send(mine, mine, *sems, (base + (here_chip + d) % count * 2 + core, col))
+                    away = count // 2 + d // 2 * (1 - 2 * (d % 2))
+                    send(mine, mine, *sems, (base + (here_chip + away) % count * 2 + core, col))
                     return _
 
             else:

time: 58.1 us -> 57.8 us (level)
  no operation moved by 1% of the time
where the time goes in v5:
time: 57.8 us; the launch traced here: 57.7 us
  Pallas kernels  56.1 us (97%)
  local copies, waits for them, and re-layouts  1.55 us (3%)
    pallas_call x1, Pallas kernels, on_device(): pl.pallas_call(functools.partial(kernel, depth, mid, cols), out_shape=jax...  56.1 us
    unnamed x1, local copies, waits for them, and re-layouts  1.55 us

profile of v5, /device:TPU:1, one launch (start us, length us, event | category | flops | bytes accessed | tf_op | source)
XLA Modules:
  0.0 57.7 jit_solution(6408063783010625119)
XLA Ops:
  0.0 56.1 %shard_map.46 = f32[7,2,16,128]{3,2,1,0:T(8,128)} custom-call(f32[7,2,64,128]{3,2,1,0:T(8,128)} %rhs.1, f32[7,2,128,128]{3,2,1,0:T(8,128)} %inv.1, bf16[6,2,4,128,128]{4,3,2,1,0:T(8,128)(2,1)} %low.1, s32[2,4,6]{2,1,0:T(4,128)} %bitcast.1), custom_call_target="tpu_custom_call" | custom-call | tf_op jit(solution)/shard_map/pallas_call | solution.py:445
  56.1 1.6 %copy.6 = f32[7,2,16,128]{3,2,1,0:T(8,128)} copy(f32[7,2,16,128]{3,2,1,0:T(8,128)} %shard_map.46) | data formatting | bytes 229376
